TPU v7x, 32 devices: a whole 2x2x4 slice. The times are simulated.
32 devices in a mesh: src: 4 (over z), snk: 4 (over x, core), sub: 2 (over y).
Axes of the slice: x: 2, y: 2, z: 4, core: 2. Of those that a mesh axis runs over, the one named last changes fastest.
Arguments:
- peram: bfloat16 [4, 4, 2, 512, 512], P('src', 'snk', None, 'sub'), may hold values from -6 to 6
- elemental: bfloat16 [2, 512, 512], replicated, may hold values from -0.0078125 to 0.0078125
- spin_signs: int32 [4], replicated, may hold values from 0 to 1
- insertions: int32 [4], replicated, may hold values from 0 to 3
Outputs:
- peram_full: bfloat16 [4, 4, 2, 512, 512], P('src', 'snk', None, 'sub')
- contraction: float32 [4, 4, 2, 512, 512], P('src', 'snk', None, 'sub')
Inputs may be any that keep to these rules, and one draw needn't show every extreme that they name: `spin_signs`: one entry for each of the four spin blocks. `insertions`: insertion times may repeat.
All inputs are finite; a program needn't handle non-finite values.
Results may differ from a plain program's by a relative error of at most 0.0029.
Values may be sent and summed in bfloat16 or wider, within the bound.
No kernel may reach another device: no remote copies, remote signals or barrier semaphores. Data moves between devices by JAX's collectives and lax.ppermute only.
A program may use at most 64 MiB of HBM per device.

v0:
```python
import jax
import jax.numpy as jnp
from jax import lax
from jax.sharding import PartitionSpec as P


def broadcast(block, axis, owner):
    block = jnp.where(lax.axis_index(axis) == owner, block, jnp.zeros_like(block))
    return lax.psum(block, axis)


def complex_product(first, second):
    real_part = jnp.dot(first[0], second[0], preferred_element_type=jnp.float32) - jnp.dot(
        first[1], second[1], preferred_element_type=jnp.float32
    )
    imag_part = jnp.dot(first[0], second[1], preferred_element_type=jnp.float32) + jnp.dot(
        first[1], second[0], preferred_element_type=jnp.float32
    )
    return jnp.stack([real_part, imag_part], axis=0)


def local(peram, elemental, spin_signs, insertions):
    n_sub = lax.axis_size("sub")
    n_snk = lax.axis_size("snk")
    own = peram[0, 0]
    rows_half = own.shape[1]
    width = own.shape[2]
    signs = 1.0 - 2.0 * jnp.repeat(spin_signs.astype(jnp.float32), width // 4)
    half_index = lax.axis_index("sub")
    col_signs = lax.dynamic_slice_in_dim(signs, half_index * rows_half, rows_half)
    flip = signs[:, None] * col_signs[None, :]
    mirror_re = flip * own[0].astype(jnp.float32).T
    mirror_im = -flip * own[1].astype(jnp.float32).T
    mirrored = jnp.stack([mirror_re, mirror_im], axis=0).astype(jnp.bfloat16)
    piece_rows = width // (n_sub * n_snk)
    outgoing = mirrored.reshape(2, n_sub, n_snk, piece_rows, rows_half)
    outgoing = outgoing.transpose(2, 1, 0, 3, 4).reshape(n_snk * n_sub, 1, 2, piece_rows, rows_half)
    spread = lax.all_to_all(outgoing, ("snk", "sub"), split_axis=0, concat_axis=1, tiled=True)
    spread = spread.reshape(n_snk, n_sub, 2, piece_rows, rows_half)
    homed = lax.all_to_all(
        lax.all_to_all(spread, "src", split_axis=0, concat_axis=0, tiled=True),
        "snk",
        split_axis=0,
        concat_axis=3,
        tiled=True,
    )
    upper = homed[0].transpose(1, 2, 0, 3).reshape(2, rows_half, width)
    row_block = lax.axis_index("src")
    col_block = lax.axis_index("snk")
    full_half = jnp.where(row_block >= col_block, own, upper)
    payload = complex_product(full_half, elemental).astype(jnp.bfloat16)
    total = jnp.zeros((2, rows_half, width), jnp.float32)
    for index in range(insertions.shape[0]):
        moment = insertions[index]
        received = broadcast(payload, "snk", moment)
        halves = []
        for part in range(n_sub):
            halves.append(broadcast(full_half, ("src", "sub"), moment * n_sub + part))
        right = jnp.concatenate(halves, axis=1)
        total = total + complex_product(received, right)
    return (full_half[None, None], total[None, None])


def solution(mesh):
    return jax.shard_map(
        local,
        mesh=mesh,
        in_specs=(P("src", "snk", None, "sub", None), P(), P(), P()),
        out_specs=(P("src", "snk", None, "sub", None), P("src", "snk", None, "sub", None)),
        check_vma=False,
    )
```

profile of v0, /device:TPU:0, one launch (start us, length us, event | category | flops | bytes accessed | tf_op | source)
XLA Modules:
  0.0 285.5 jit_solution(458601436078374853)
XLA Ops:
  7.2 1.2 copy.28
  8.9 13.8 %all_to_all.29 = bf16[8,1,2,64,256]{4,3,2,1,0:T(8,128)(2,1)S(1)} all-to-all(bf16[8,1,2,64,256]{4,3,2,1,0:T(8,128)(2,1)S(1)} %bitcast.150), channel_id=1, replica_groups=mesh['src'=4,'snk'=4,'sub'=2] {'snk','sub'}, dimensions={0} | all-to-all | bytes 1048576 | tf_op jit(solution)/shard_map/all_to_all | solution.py:38
  22.7 19.8 %all_to_all.30 = bf16[4,2,2,64,256]{4,3,2,1,0:T(8,128)(2,1)} all-to-all(bf16[4,2,2,64,256]{4,3,2,1,0:T(8,128)(2,1)S(1)} %bitcast.151), channel_id=1, replica_groups=mesh['src'=4,'snk'=4,'sub'=2] {'src'}, dimensions={0} | all-to-all | bytes 1048576 | tf_op jit(solution)/shard_map/all_to_all | solution.py:41
  42.5 3.5 %all-to-all-start.2 = ((bf16[4,2,2,64,256]{4,3,2,1,0:T(8,128)(2,1)}), bf16[4,2,2,64,256]{4,3,2,1,0:T(8,128)(2,1)S(1)}, u32[]{:S(2)}, u32[]{:S(2)}) async-start(bf16[4,2,2,64,256]{4,3,2,1,0:T(8,128)(2,1)} %all_to_all.30), calls=%async_computation.2 | async-start | bytes 1048576 | tf_op jit(solution)/shard_map/all_to_all | solution.py:40
  46.0 0.6 copy-done.13
  46.7 0.7 fusion.35
  50.0 4.8 %all-to-all-done.2 = bf16[4,2,2,64,256]{4,3,2,1,0:T(8,128)(2,1)S(1)} async-done(((bf16[4,2,2,64,256]{4,3,2,1,0:T(8,128)(2,1)}), bf16[4,2,2,64,256]{4,3,2,1,0:T(8,128)(2,1)S(1)}, u32[]{:S(2)}, u32[]{:S(2)}) %all-to-all-start.2) | async-done | bytes 524320 | tf_op jit(solution)/shard_map/all_to_all | solution.py:40
  54.9 1.0 copy-done.5
  55.9 0.9 broadcast_select_fusion
  56.7 1.9 broadcast_select_fusion.1
  61.6 0.3 fusion.10
  62.2 0.3 fusion.11
  62.5 1.4 broadcast_select_fusion.2
  64.2 1.0 copy.30
  65.2 147.6 %all-reduce.5.cloned.1.call-done = (bf16[2,256,512]{2,1,0:T(8,128)(2,1)}, bf16[2,256,512]{2,1,0:T(8,128)(2,1)}, bf16[2,256,512]{2,1,0:T(8,128)(2,1)}, bf16[2,256...) async-done(((bf16[2,256,512]{2,1,0:T(8,128)(2,1)}, ...) | async-done | bytes 4194320 | tf_op jit(solution)/shard_map/psum | solution.py:9
  212.8 1.1 constant_dynamic-update-slice_fusion.1
  214.1 1.0 copy-done.11
  215.3 50.5 %all-reduce.7.cloned.1.call-done = (bf16[2,256,512]{2,1,0:T(8,128)(2,1)}, bf16[2,256,512]{2,1,0:T(8,128)(2,1)}, bf16[2,256,512]{2,1,0:T(8,128)(2,1)}, bf16[2,256,512]{2,1,0:T(8,128)(2,1)}) async-done(((bf16[2,256,512]{2,1,0:T(8,128)(2,1)}, bf16[2,256,512]{2,1,0:T(8,128)(2,1)}, bf16[2,256,512]{2,1,0:T(8,128)(2,1)}, bf16[2,256,512]{2,1,0:T(8,128)(2,1)}), (bf16[2,256,512]{2,1,0:T(8,128)(2,1)}, ...) | async-done | bytes 2097168 | tf_op jit(solution)/shard_map/psum | solution.py:9
  265.8 1.3 fusion.24
  267.4 0.7 copy-done.3
  268.8 0.7 copy-done.7
  269.5 1.0 copy-done.6
  270.6 1.0 copy-done.9
  271.8 0.9 copy-done.2
  273.4 0.7 copy-done.1
  274.7 0.3 fusion.6
  275.3 0.3 fusion.4
  275.6 0.3 fusion.5
  276.3 0.3 fusion.3
  276.6 0.3 fusion
  276.9 0.3 fusion.1
  277.2 1.5 fusion.13
  (51 shorter events, 4.8 us)
Async XLA Ops:
  7.2 1.3 copy-start.14
  42.5 12.3 %all-to-all-start.2 = ((bf16[4,2,2,64,256]{4,3,2,1,0:T(8,128)(2,1)}), bf16[4,2,2,64,256]{4,3,2,1,0:T(8,128)(2,1)S(1)}, u32[]{:S(2)}, u32[]{:S(2)}) async-start(bf16[4,2,2,64,256]{4,3,2,1,0:T(8,128)(2,1)} %all_to_all.30), calls=%async_computation.2 | async-start | bytes 1048576 | tf_op jit(solution)/shard_map/all_to_all | solution.py:40
  46.0 166.9 %all-reduce.5.cloned.1.call-start = ((), (), s32[]{:S(2)}) async-start(), calls=%async_computation.3 | async-start | bytes 8388608 | tf_op jit(solution)/shard_map/psum | solution.py:9
  46.0 0.7 copy-start.13
  54.8 1.0 copy-start.5
  58.6 2.7 copy-start
  58.6 207.2 %all-reduce.7.cloned.1.call-start = ((), (), s32[]{:S(2)}) async-start(), calls=%async_computation.4 | async-start | bytes 4194304 | tf_op jit(solution)/shard_map/psum | solution.py:9
  212.8 1.2 copy-start.8
  214.0 1.0 copy-start.11
  214.0 1.2 copy-start.12
  265.8 1.3 copy-start.4
  267.1 1.0 copy-start.3
  268.4 1.0 copy-start.7
  269.5 1.0 copy-start.6
  270.5 1.0 copy-start.9
  270.5 1.2 copy-start.10
  271.7 1.0 copy-start.2
  273.1 1.0 copy-start.1
Sparse Core Ops, SparseCore 0:
  58.7 154.0 all-reduce.4
  215.4 50.3 all-reduce.6
where the time goes:
time: 286 us; the launch traced here: 285 us
  waiting for transfers between devices  203 us (71%)
  blocking collectives  33.6 us (12%)
  between operations  19.7 us (7%)
  local copies, waits for them, and re-layouts  13 us (5%)
  matrix products  6.95 us (2%)
  other arithmetic  5.86 us (2%)
  starting transfers between devices  3.55 us (1%)
    psum x2, waiting for transfers between devices, broadcast(): return lax.psum(block, axis)  198 us
    all_to_all x1, blocking collectives, local(): lax.all_to_all(spread, 'src', split_axis=0, concat_axis=0, tiled=True)  19.8 us
    all_to_all x1, blocking collectives, local(): lax.all_to_all(outgoing, ('snk', 'sub'), split_axis=0, concat_axis=1, til...  13.8 us
    unnamed x36, local copies, waits for them, and re-layouts  11.7 us
  transfers between devices with their start and end apart: 3, of which 3 were waited for; matrix products, arithmetic and copies ran while one was open for 2% of the time, Pallas kernels for 0%

commit v1 on v0

--- a/solution.py
+++ b/solution.py
@@ -6,7 +6,7 @@
 
 def broadcast(block, axis, owner):
     block = jnp.where(lax.axis_index(axis) == owner, block, jnp.zeros_like(block))
-    return lax.psum(block, axis)
+    return jnp.sum(lax.all_gather(block, axis), axis=0)
 
 
 def complex_product(first, second):

time: 286 us -> 759 us (2.65)
  waiting for transfers between devices: 203 us -> 636 us
  other arithmetic: 5.86 us -> 42.5 us
  matrix products: 6.95 us -> 17.5 us
  local copies, waits for them, and re-layouts: 13 us -> 4.22 us
    all_gather x0 -> x12, waiting for transfers between devices: none -> 625 us  [broadcast(): return jnp.sum(lax.all_gather(block, axis), axis=0)]
    psum x2 -> x0, waiting for transfers between devices: 198 us -> none  [broadcast(): return lax.psum(block, axis)]
    reduce_sum x0 -> x12, other arithmetic: none -> 35.8 us  [broadcast(): return jnp.sum(lax.all_gather(block, axis), axis=0)]
    unnamed x36, local copies, waits for them, and re-layouts: 11.7 us -> 2.32 us
  transfers between devices with their start and end apart: 3 -> 13, of which waited for: 3 -> 13; matrix products, arithmetic and copies ran while one was open for 2% -> 6% of each run, Pallas kernels for 0% -> 0%
where the time goes in v1:
time: 759 us; the launch traced here: 758 us
  waiting for transfers between devices  636 us (84%)
  other arithmetic  42.5 us (6%)
  blocking collectives  33.7 us (4%)
  between operations  19.5 us (3%)
  matrix products  17.5 us (2%)
    all_gather x12, waiting for transfers between devices, broadcast(): return jnp.sum(lax.all_gather(block, axis), axis=0)  625 us
    reduce_sum x12, other arithmetic, broadcast(): return jnp.sum(lax.all_gather(block, axis), axis=0)  35.8 us
    all_to_all x1, blocking collectives, local(): lax.all_to_all(spread, 'src', split_axis=0, concat_axis=0, tiled=True)  19.8 us
  transfers between devices with their start and end apart: 13, of which 13 were waited for; matrix products, arithmetic and copies ran while one was open for 6% of the time, Pallas kernels for 0%

profile of v1, /device:TPU:0, one launch (start us, length us, event | category | flops | bytes accessed | tf_op | source)
XLA Modules:
  0.0 757.7 jit_solution(4344423147505105243)
XLA Ops:
  9.5 13.9 %all_to_all.29 = bf16[8,1,2,64,256]{4,3,2,1,0:T(8,128)(2,1)S(1)} all-to-all(bf16[8,1,2,64,256]{4,3,2,1,0:T(8,128)(2,1)S(1)} %bitcast.152), channel_id=1, replica_groups=mesh['src'=4,'snk'=4,'sub'=2] {'snk','sub'}, dimensions={0} | all-to-all | bytes 1048576 | tf_op jit(solution)/shard_map/all_to_all | solution.py:38
  23.5 19.8 %all_to_all.30 = bf16[4,2,2,64,256]{4,3,2,1,0:T(8,128)(2,1)} all-to-all(bf16[4,2,2,64,256]{4,3,2,1,0:T(8,128)(2,1)S(1)} %bitcast.153), channel_id=1, replica_groups=mesh['src'=4,'snk'=4,'sub'=2] {'src'}, dimensions={0} | all-to-all | bytes 1048576 | tf_op jit(solution)/shard_map/all_to_all | solution.py:41
  43.3 3.5 all-to-all-start.2
  49.8 5.7 all-to-all-done.2
  65.0 1.9 broadcast_select_fusion
  72.1 6.5 all-gather.31.cloned.1.call-done
  78.6 2.9 reduce_sum.153
  81.5 21.3 %all-gather.19.cloned.1.call-done = bf16[4,2,256,512]{3,2,1,0:T(8,128)(2,1)} async-done(((bf16[1,2,256,512]{3,2,1,0:T(8,128)(2,1)}), bf16[4,2,256,512]{3,2,1,0:T(8,128)(2,1)}) %all-gather.19.cloned.1.call-update) | async-done | bytes 2097168 | tf_op jit(solution)/shard_map/all_gather | solution.py:9
  102.8 2.9 reduce_sum.147
  105.6 21.3 %all-gather.25.cloned.1.call-done = bf16[4,2,256,512]{3,2,1,0:T(8,128)(2,1)} async-done(((bf16[1,2,256,512]{3,2,1,0:T(8,128)(2,1)}), bf16[4,2,256,512]{3,2,1,0:T(8,128)(2,1)}) %all-gather.25.cloned.1.call-update) | async-done | bytes 2097168 | tf_op jit(solution)/shard_map/all_gather | solution.py:9
  126.9 2.8 reduce_sum.150
  129.8 21.2 %all-gather.13.cloned.1.call-done = bf16[4,2,256,512]{3,2,1,0:T(8,128)(2,1)} async-done(((bf16[1,2,256,512]{3,2,1,0:T(8,128)(2,1)}), bf16[4,2,256,512]{3,2,1,0:T(8,128)(2,1)}) %all-gather.13.cloned.1.call-update) | async-done | bytes 2097168 | tf_op jit(solution)/shard_map/all_gather | solution.py:9
  150.9 2.9 reduce_sum.144
  153.8 71.9 %all-gather.33.cloned.1.call-done = bf16[8,2,256,512]{3,2,1,0:T(8,128)(2,1)} async-done(((bf16[1,2,256,512]{3,2,1,0:T(8,128)(2,1)}), bf16[8,2,256,512]{3,2,1,0:T(8,128)(2,1)}) %all-gather.33.cloned.1.call-update) | async-done | bytes 4194320 | tf_op jit(solution)/shard_map/all_gather | solution.py:9
  225.7 3.0 reduce_sum.154
  228.7 70.4 %all-gather.29.cloned.1.call-done = bf16[8,2,256,512]{3,2,1,0:T(8,128)(2,1)} async-done(((bf16[1,2,256,512]{3,2,1,0:T(8,128)(2,1)}), bf16[8,2,256,512]{3,2,1,0:T(8,128)(2,1)}) %all-gather.29.cloned.1.call-update) | async-done | bytes 4194320 | tf_op jit(solution)/shard_map/all_gather | solution.py:9
  299.1 3.0 reduce_sum.152
  302.0 70.5 %all-gather.27.cloned.1.call-done = bf16[8,2,256,512]{3,2,1,0:T(8,128)(2,1)} async-done(((bf16[1,2,256,512]{3,2,1,0:T(8,128)(2,1)}), bf16[8,2,256,512]{3,2,1,0:T(8,128)(2,1)}) %all-gather.27.cloned.1.call-update) | async-done | bytes 4194320 | tf_op jit(solution)/shard_map/all_gather | solution.py:9
  372.6 3.0 reduce_sum.151
  375.5 70.5 %all-gather.23.cloned.1.call-done = bf16[8,2,256,512]{3,2,1,0:T(8,128)(2,1)} async-done(((bf16[1,2,256,512]{3,2,1,0:T(8,128)(2,1)}), bf16[8,2,256,512]{3,2,1,0:T(8,128)(2,1)}) %all-gather.23.cloned.1.call-update) | async-done | bytes 4194320 | tf_op jit(solution)/shard_map/all_gather | solution.py:9
  446.0 3.0 reduce_sum.149
  449.0 70.5 %all-gather.21.cloned.1.call-done = bf16[8,2,256,512]{3,2,1,0:T(8,128)(2,1)} async-done(((bf16[1,2,256,512]{3,2,1,0:T(8,128)(2,1)}), bf16[8,2,256,512]{3,2,1,0:T(8,128)(2,1)}) %all-gather.21.cloned.1.call-update) | async-done | bytes 4194320 | tf_op jit(solution)/shard_map/all_gather | solution.py:9
  519.5 3.0 reduce_sum.148
  522.5 70.4 %all-gather.17.cloned.1.call-done = bf16[8,2,256,512]{3,2,1,0:T(8,128)(2,1)} async-done(((bf16[1,2,256,512]{3,2,1,0:T(8,128)(2,1)}), bf16[8,2,256,512]{3,2,1,0:T(8,128)(2,1)}) %all-gather.17.cloned.1.call-update) | async-done | bytes 4194320 | tf_op jit(solution)/shard_map/all_gather | solution.py:9
  592.9 3.0 reduce_sum.146
  595.8 70.5 %all-gather.15.cloned.1.call-done = bf16[8,2,256,512]{3,2,1,0:T(8,128)(2,1)} async-done(((bf16[1,2,256,512]{3,2,1,0:T(8,128)(2,1)}), bf16[8,2,256,512]{3,2,1,0:T(8,128)(2,1)}) %all-gather.15.cloned.1.call-update) | async-done | bytes 4194320 | tf_op jit(solution)/shard_map/all_gather | solution.py:9
  666.4 3.7 reduce_sum.145
  670.1 2.2 fusion.39
  672.3 2.1 fusion.40
  674.5 2.1 fusion.41
  679.9 59.8 %all-gather.35.cloned.1.call-done = bf16[8,2,256,512]{3,2,1,0:T(8,128)(2,1)} async-done(((bf16[1,2,256,512]{3,2,1,0:T(8,128)(2,1)}), bf16[8,2,256,512]{3,2,1,0:T(8,128)(2,1)}) %all-gather.35.cloned.1.call-update) | async-done | bytes 4194320 | tf_op jit(solution)/shard_map/all_gather | solution.py:9
  739.7 3.0 reduce_sum.155
  (93 shorter events, 26.3 us)
Async XLA Ops:
  7.2 39.6 %copy-start.16 = (s32[4]{0:T(128)S(1)}, s32[4]{0:T(128)}, u32[]{:S(2)}) copy-start(s32[4]{0:T(128)} %param.7) | copy-start | bytes 52
  9.5 46.4 %copy-start.3 = (bf16[2,512,512]{2,1,0:T(8,128)(2,1)S(1)}, bf16[2,512,512]{2,1,0:T(8,128)(2,1)}, u32[]{:S(2)}) copy-start(bf16[2,512,512]{2,1,0:T(8,128)(2,1)} %param.5) | copy-start | bytes 3145732
  43.3 12.3 %all-to-all-start.2 = ((bf16[4,2,2,64,256]{4,3,2,1,0:T(8,128)(2,1)}), bf16[4,2,2,64,256]{4,3,2,1,0:T(8,128)(2,1)S(1)}, u32[]{:S(2)}, u32[]{:S(2)}) async-start(bf16[4,2,2,64,256]{4,3,2,1,0:T(8,128)(2,1)} %all_to_all.30), calls=%async_computation.2 | async-start | bytes 1048576 | tf_op jit(solution)/shard_map/all_to_all | solution.py:40
  46.8 31.9 %all-gather.31.cloned.1.call-start = ((), (), s32[]{:S(2)}) async-start(), calls=%async_computation.12 | async-start | bytes 2621440 | tf_op jit(solution)/shard_map/all_gather | solution.py:9
  56.9 5.4 copy-start.12
  58.6 44.2 %all-gather.19.cloned.1.call-start = ((), (), s32[]{:S(2)}) async-start(), calls=%async_computation.6 | async-start | bytes 2621440 | tf_op jit(solution)/shard_map/all_gather | solution.py:9
  59.4 67.6 %all-gather.25.cloned.1.call-start = ((), (), s32[]{:S(2)}) async-start(), calls=%async_computation.9 | async-start | bytes 2621440 | tf_op jit(solution)/shard_map/all_gather | solution.py:9
  60.1 90.8 %all-gather.13.cloned.1.call-start = ((), (), s32[]{:S(2)}) async-start(), calls=%async_computation.3 | async-start | bytes 2621440 | tf_op jit(solution)/shard_map/all_gather | solution.py:9
  60.7 165.1 %all-gather.33.cloned.1.call-start = ((), (), s32[]{:S(2)}) async-start(), calls=%async_computation.13 | async-start | bytes 4718592 | tf_op jit(solution)/shard_map/all_gather | solution.py:9
  63.2 235.9 %all-gather.29.cloned.1.call-start = ((), (), s32[]{:S(2)}) async-start(), calls=%async_computation.11 | async-start | bytes 4718592 | tf_op jit(solution)/shard_map/all_gather | solution.py:9
  66.9 305.6 %all-gather.27.cloned.1.call-start = ((), (), s32[]{:S(2)}) async-start(), calls=%async_computation.10 | async-start | bytes 4718592 | tf_op jit(solution)/shard_map/all_gather | solution.py:9
  67.7 378.4 %all-gather.23.cloned.1.call-start = ((), (), s32[]{:S(2)}) async-start(), calls=%async_computation.8 | async-start | bytes 4718592 | tf_op jit(solution)/shard_map/all_gather | solution.py:9
  68.4 451.1 %all-gather.21.cloned.1.call-start = ((), (), s32[]{:S(2)}) async-start(), calls=%async_computation.7 | async-start | bytes 4718592 | tf_op jit(solution)/shard_map/all_gather | solution.py:9
  69.2 523.7 %all-gather.17.cloned.1.call-start = ((), (), s32[]{:S(2)}) async-start(), calls=%async_computation.5 | async-start | bytes 4718592 | tf_op jit(solution)/shard_map/all_gather | solution.py:9
  69.7 596.6 %all-gather.15.cloned.1.call-start = ((), (), s32[]{:S(2)}) async-start(), calls=%async_computation.4 | async-start | bytes 4718592 | tf_op jit(solution)/shard_map/all_gather | solution.py:9
  70.5 669.2 %all-gather.35.cloned.1.call-start = ((), (), s32[]{:S(2)}) async-start(), calls=%async_computation.14 | async-start | bytes 4718592 | tf_op jit(solution)/shard_map/all_gather | solution.py:9
  595.8 78.6 %copy-start = (bf16[2,256,512]{2,1,0:T(8,128)(2,1)}, bf16[2,256,512]{2,1,0:T(8,128)(2,1)S(1)}, u32[]{:S(2)}) copy-start(bf16[2,256,512]{2,1,0:T(8,128)(2,1)S(1)} %reduce_sum.146) | copy-start | bytes 1572868
  670.1 6.5 copy-start.7
  670.1 7.6 copy-start.5
  742.7 4.5 copy-start.1
  742.7 4.5 copy-start.2
  742.7 4.5 copy-start.9
  742.7 4.5 copy-start.15
  742.7 4.8 copy-start.8
  742.7 4.8 copy-start.11
  744.1 3.7 copy-start.14
  745.4 2.7 copy-start.6
  745.4 2.7 copy-start.10
  747.2 1.3 copy-start.13
  747.5 1.3 copy-start.4
Sparse Core Ops, SparseCore 0:
  58.7 19.8 all-gather.30
  80.2 22.5 all-gather.18
  104.3 22.5 all-gather.24
  128.3 22.5 all-gather.12
  152.9 72.7 all-gather.32
  227.7 71.3 all-gather.28
  301.2 71.3 all-gather.26
  374.7 71.3 all-gather.22
  448.2 71.3 all-gather.20
  521.5 71.3 all-gather.16
  595.0 71.3 all-gather.14
  668.3 71.3 all-gather.34
